TPU v7x, 256 devices: a whole 4x4x8 slice. The times are simulated.
256 devices in a mesh: seq: 64 (over x, z_hi, y, core), chan: 4 (over z_lo).
Axes of the slice: x: 4, y: 4, z: 8 (z_hi: 2, z_lo: 4; z = z_hi * 4 + z_lo), core: 2. Of those that a mesh axis runs over, the one named last changes fastest.
Arguments:
- signal: bfloat16 [1024, 16384], P('chan', 'seq'), may hold values from -6 to 6
- gating: bfloat16 [1024, 16384], P('chan', 'seq'), may hold values from -6 to 6
- filter_taps: float32 [1024, 16384], P('chan', 'seq'), may hold values from -6 to 6
- decay_rates: float32 [1024], P('chan'), may hold values from 1.5258789e-05 to 0.0009765625
- out_weight: bfloat16 [1024, 2048], P(None, 'chan'), may hold values from -0.1875 to 0.1875
- out_grad: bfloat16 [16384, 2048], P('seq', 'chan'), may hold values from -1.5 to 1.5
Outputs:
- mixed_out: bfloat16 [16384, 2048], P('seq', 'chan')
- signal_grad: float32 [1024, 16384], P('chan', 'seq')
- gating_grad: float32 [1024, 16384], P('chan', 'seq')
- taps_grad: float32 [1024, 16384], P('chan', 'seq')
All inputs are finite; a program needn't handle non-finite values.
Results may differ from a plain program's by a relative error of at most 0.013.
Values may be sent and summed in bfloat16 or wider, within the bound.
A program may use at most 64 MiB of HBM per device.

v0:
```python
import functools

import jax
import jax.numpy as jnp
import numpy as np
from jax import lax
from jax.experimental import pallas as pl
from jax.experimental.pallas import tpu as pltpu
from jax.sharding import PartitionSpec as P

F32, BF16 = jnp.float32, jnp.bfloat16
MESH = pl.DeviceIdType.MESH
LANES = 128


def halves(table):
    high = table.astype(BF16)
    return high, (table - high.astype(np.float64)).astype(BF16)


def tables(shards, folds):
    rows = shards * folds
    length = rows * LANES
    freq = 2 * np.arange(rows)[:, None] + 1
    order = np.arange(rows)
    coarse = folds * (order % shards) + order // shards
    angle = 2 * np.pi * (freq * coarse[None, :] % (4 * rows)) / (4 * rows)
    first = np.concatenate([np.cos(angle), -np.sin(angle)], 0)
    fine = np.arange(LANES)
    turn = 2 * np.pi * (freq * fine[None, :]) / (4 * length)
    inner = 2 * np.pi * (fine[:, None] * fine[None, :] % LANES) / LANES
    re, im = np.cos(inner), -np.sin(inner)
    ahead = np.block([[re, im], [-im, re]])
    back = np.block([[re, -im], [im, re]])
    first_high, first_low = halves(first)
    last_high, last_low = halves(first.T / length)
    return (
        np.concatenate([first_high, first_low], 1),
        last_high,
        last_low,
        *halves(ahead),
        *halves(back),
        np.cos(turn).astype(np.float32),
        (-np.sin(turn)).astype(np.float32),
    )


def split(value):
    high = value.astype(BF16)
    return high, (value - high.astype(F32)).astype(BF16)


def mm(left, right):
    return jnp.dot(left, right, preferred_element_type=F32)


def body(
    shards, chans,
    sig_ref, gate_ref, taps_ref, decay_ref, weight_ref, og_ref,
    first_ref, lasth_ref, lastl_ref, fwdh_ref, fwdl_ref, bckh_ref, bckl_ref, cos_ref, sin_ref,
    out_ref, sgrad_ref, ggrad_ref, tgrad_ref,
    in_send, in_recv, rs_send, rs_recv, mx_send, mx_recv, gr_send, gr_recv, rt_send, rt_recv, ag_send, ag_recv,
    rows, window, grad_out, xcat, bh, bl, spec, zh, zl,
    sends, recvs,
):
    me, ch = lax.axis_index("seq"), lax.axis_index("chan")
    far = lax.rem(ch + chans // 2, chans)
    wide, span = sig_ref.shape
    folds = span // LANES
    mine = wide // shards
    n1 = shards * folds

    barrier = pltpu.get_barrier_semaphore()

    @pl.loop(0, shards)
    def _(i):
        pl.semaphore_signal(barrier, inc=1, device_id=(i, far), device_id_type=MESH)

    near = [k for k in range(1, chans) if k != chans // 2]
    for k in near:
        pl.semaphore_signal(barrier, inc=1, device_id=(me, lax.rem(ch + k, chans)), device_id_type=MESH)

    def to_rows(value):
        for h in range(folds):
            rows[pl.ds(h, wide, stride=folds), :] = value[:, h * LANES : (h + 1) * LANES]
        return rows[...].reshape(shards, mine * folds, LANES).astype(BF16)

    def from_rows(block):
        rows[...] = block.astype(F32).reshape(wide * folds, LANES)
        return [rows[pl.ds(h, wide, stride=folds), :] for h in range(folds)]

    def spread(source, target, k):
        @pl.loop(0, shards)
        def _(i):
            peer = lax.rem(me + i, shards)
            pltpu.make_async_remote_copy(
                source.at[peer], target.at[me], sends.at[k], recvs.at[k],
                device_id=(peer, far), device_id_type=MESH,
            ).start()

    def joint(source, target, k):
        return pltpu.make_async_remote_copy(
            source, target, sends.at[k], recvs.at[k], device_id=(me, far), device_id_type=MESH
        )

    place = lax.broadcasted_iota(jnp.int32, (1, span), 1) + me * span
    place = place.astype(F32)
    for i in range(wide // LANES):
        row = decay_ref[i : i + 1, :]
        rate = jnp.transpose(jnp.broadcast_to(row, (LANES, LANES)))
        size = jnp.sqrt(2.0 * rate)
        for h in range(folds):
            cols = slice(h * LANES, (h + 1) * LANES)
            window[i * LANES : (i + 1) * LANES, cols] = jnp.exp(-rate * place[:, cols]) * size

    in_send[:, 0] = to_rows(sig_ref[...].astype(F32))
    in_send[:, 1] = to_rows(taps_ref[...] * window[...])

    pl.semaphore_wait(barrier, shards + len(near))
    spread(in_send, in_recv, 0)

    def share(k):
        block = lax.rem(ch + k, chans)
        part = weight_ref[pl.ds(pl.multiple_of(block * wide, wide), wide), :]
        return lax.dot_general(part, og_ref[...], (((1,), (1,)), ((), ())), preferred_element_type=F32)

    for k in range(1, chans):
        rs_send[k - 1] = share(k).astype(BF16)
        pltpu.make_async_remote_copy(
            rs_send.at[k - 1], rs_recv.at[k - 1], sends.at[1], recvs.at[1],
            device_id=(me, lax.rem(ch + k, chans)), device_id_type=MESH,
        ).start()
    grad_out[...] = share(0).astype(BF16).astype(F32)

    cosine, sine = cos_ref[...], sin_ref[...]

    def analyse(block, base):
        rows[...] = block.astype(F32).reshape(wide * folds, LANES)
        for c in range(mine):
            column = jnp.concatenate(
                [rows[pl.ds(c * folds + h, shards, stride=mine * folds), :] for h in range(folds)], 0
            ).astype(BF16)
            cols = slice(c * LANES, (c + 1) * LANES)
            xcat[:n1, cols] = column
            xcat[n1:, cols] = column
        stage = mm(first_ref[...], xcat[...])
        for c in range(mine):
            cols = slice(c * LANES, (c + 1) * LANES)
            real, imag = stage[:n1, cols], stage[n1:, cols]
            turned = jnp.concatenate([real * cosine - imag * sine, real * sine + imag * cosine], 1)
            bh[c * n1 : (c + 1) * n1], bl[c * n1 : (c + 1) * n1] = split(turned)
        high, low = bh[...], bl[...]
        spec[base] = mm(high, fwdh_ref[...]) + mm(low, fwdh_ref[...]) + mm(high, fwdl_ref[...])

    def synthesize(real, imag):
        high, low = split(jnp.concatenate([real, imag], 1))
        stage = mm(high, bckh_ref[...]) + mm(low, bckh_ref[...]) + mm(high, bckl_ref[...])
        for c in range(mine):
            part = stage[c * n1 : (c + 1) * n1]
            real, imag = part[:, :LANES], part[:, LANES:]
            turned = jnp.concatenate([real * cosine + imag * sine, imag * cosine - real * sine], 0)
            cols = slice(c * LANES, (c + 1) * LANES)
            zh[:, cols], zl[:, cols] = split(turned)
        high, low = zh[...], zl[...]
        result = mm(lasth_ref[...], high) + mm(lasth_ref[...], low) + mm(lastl_ref[...], high)
        for c in range(mine):
            for h in range(folds):
                rows[pl.ds(c * folds + h, shards, stride=mine * folds), :] = result[
                    h * shards : (h + 1) * shards, c * LANES : (c + 1) * LANES
                ]
        return rows[...].reshape(shards, mine * folds, LANES).astype(BF16)

    def parts(k):
        return spec[k, :, :LANES], spec[k, :, LANES:]

    joint(in_send, in_recv, 0).wait_recv()
    analyse(in_recv[:, 0], 0)
    analyse(in_recv[:, 1], 1)
    (sr, si), (fr, fi) = parts(0), parts(1)
    mx_send[...] = synthesize(sr * fr - si * fi, sr * fi + si * fr)
    spread(mx_send, mx_recv, 2)

    joint(rs_send, rs_recv, 1).wait_recv()
    total = grad_out[...]
    for k in range(chans - 1):
        total = total + rs_recv[k].astype(F32)
    grad_out[...] = total
    gr_send[...] = to_rows(total * gate_ref[...].astype(F32))
    spread(gr_send, gr_recv, 3)

    joint(mx_send, mx_recv, 2).wait_recv()
    mixed = jnp.concatenate(from_rows(mx_recv[...]), 1)
    ag_send[...] = jnp.transpose(mixed * gate_ref[...].astype(F32)).astype(BF16)
    for k in range(1, chans):
        pltpu.make_async_remote_copy(
            ag_send, ag_recv.at[k - 1], sends.at[4], recvs.at[4],
            device_id=(me, lax.rem(ch + k, chans)), device_id_type=MESH,
        ).start()
    ggrad_ref[...] = grad_out[...] * mixed

    joint(gr_send, gr_recv, 3).wait_recv()
    analyse(gr_recv[...], 2)
    gr, gi = parts(2)
    fr, fi = parts(1)
    rt_send[:, 0] = synthesize(gr * fr + gi * fi, gi * fr - gr * fi)
    sr, si = parts(0)
    gr, gi = parts(2)
    rt_send[:, 1] = synthesize(gr * sr + gi * si, gi * sr - gr * si)
    spread(rt_send, rt_recv, 5)

    def project(block, gathered):
        part = weight_ref[pl.ds(pl.multiple_of(block * wide, wide), wide), :]
        return mm(gathered, part)

    joint(ag_recv, ag_recv, 4).wait_recv()
    total = project(ch, ag_send[...])
    for k in range(1, chans):
        total = total + project(lax.rem(ch + chans - k, chans), ag_recv[k - 1])
    out_ref[...] = total.astype(BF16)

    joint(rt_send, rt_recv, 5).wait_recv()
    for h, value in enumerate(from_rows(rt_recv[:, 0])):
        sgrad_ref[:, h * LANES : (h + 1) * LANES] = value
    for h, value in enumerate(from_rows(rt_recv[:, 1])):
        cols = slice(h * LANES, (h + 1) * LANES)
        tgrad_ref[:, cols] = value * window[:, cols]

    joint(in_send, in_recv, 0).wait_send()
    joint(rs_send, rs_recv, 1).wait_send()
    joint(mx_send, mx_recv, 2).wait_send()
    joint(gr_send, gr_recv, 3).wait_send()
    joint(ag_recv, ag_recv, 4).wait_send()
    joint(rt_send, rt_recv, 5).wait_send()


def per_device(shards, chans, consts, signal, gating, filter_taps, decay_rates, out_weight, out_grad):
    wide, span = signal.shape
    folds = span // LANES
    mine = wide // shards
    n1 = shards * folds
    tile = (mine * folds, LANES)
    vmem = pl.BlockSpec(memory_space=pltpu.VMEM)
    return pl.pallas_call(
        functools.partial(body, shards, chans),
        out_shape=(
            jax.ShapeDtypeStruct(out_grad.shape, BF16),
            jax.ShapeDtypeStruct(signal.shape, F32),
            jax.ShapeDtypeStruct(signal.shape, F32),
            jax.ShapeDtypeStruct(signal.shape, F32),
        ),
        in_specs=[vmem] * (6 + len(consts)),
        out_specs=(vmem,) * 4,
        scratch_shapes=[
            pltpu.VMEM((shards, 2, *tile), BF16),
            pltpu.VMEM((shards, 2, *tile), BF16),
            pltpu.VMEM((chans - 1, wide, span), BF16),
            pltpu.VMEM((chans - 1, wide, span), BF16),
            pltpu.VMEM((shards, *tile), BF16),
            pltpu.VMEM((shards, *tile), BF16),
            pltpu.VMEM((shards, *tile), BF16),
            pltpu.VMEM((shards, *tile), BF16),
            pltpu.VMEM((shards, 2, *tile), BF16),
            pltpu.VMEM((shards, 2, *tile), BF16),
            pltpu.VMEM((span, wide), BF16),
            pltpu.VMEM((chans - 1, span, wide), BF16),
            pltpu.VMEM((wide * folds, LANES), F32),
            pltpu.VMEM((wide, span), F32),
            pltpu.VMEM((wide, span), F32),
            pltpu.VMEM((2 * n1, mine * LANES), BF16),
            pltpu.VMEM((mine * n1, 2 * LANES), BF16),
            pltpu.VMEM((mine * n1, 2 * LANES), BF16),
            pltpu.VMEM((3, mine * n1, 2 * LANES), F32),
            pltpu.VMEM((2 * n1, mine * LANES), BF16),
            pltpu.VMEM((2 * n1, mine * LANES), BF16),
            pltpu.SemaphoreType.DMA((6,)),
            pltpu.SemaphoreType.DMA((6,)),
        ],
        compiler_params=pltpu.CompilerParams(collective_id=0, has_side_effects=True, vmem_limit_bytes=48 << 20),
    )(
        signal, gating, filter_taps, decay_rates.reshape(-1, LANES), out_weight, out_grad, *map(jnp.asarray, consts)
    )


def solution(mesh):
    shards, chans = mesh.shape["seq"], mesh.shape["chan"]

    def step(signal, gating, filter_taps, decay_rates, out_weight, out_grad):
        consts = tables(shards, signal.shape[1] // shards // LANES)
        return jax.shard_map(
            functools.partial(per_device, shards, chans, consts),
            mesh=mesh,
            in_specs=(
                P("chan", "seq"),
                P("chan", "seq"),
                P("chan", "seq"),
                P("chan"),
                P(None, "chan"),
                P("seq", "chan"),
            ),
            out_specs=(P("seq", "chan"), P("chan", "seq"), P("chan", "seq"), P("chan", "seq")),
            check_vma=False,
        )(signal, gating, filter_taps, decay_rates, out_weight, out_grad)

    return step
```

profile of v0, /device:TPU:1, one launch (start us, length us, event | category | flops | bytes accessed | tf_op | source)
XLA Modules:
  0.0 74.0 jit_solution(11264754789738178851)
XLA Ops:
  0.6 0.0 copy-start.14
  0.6 0.7 copy-done.14
  1.3 0.0 copy-start
  1.3 1.2 %copy-done = bf16[1024,512]{1,0:T(8,128)(2,1)S(1)} copy-done((bf16[1024,512]{1,0:T(8,128)(2,1)S(1)}, bf16[1024,512]{1,0:T(8,128)(2,1)}, u32[]{:S(2)}) %copy-start) | copy-done | bytes 1048600
  2.5 0.0 copy-start.1
  2.5 0.9 %copy-done.1 = f32[256,256]{1,0:T(8,128)S(1)} copy-done((f32[256,256]{1,0:T(8,128)S(1)}, f32[256,256]{1,0:T(8,128)}, u32[]{:S(2)}) %copy-start.1) | copy-done | bytes 262168
  3.5 0.0 copy-start.2
  3.5 0.9 %copy-done.2 = bf16[256,512]{1,0:T(8,128)(2,1)S(1)} copy-done((bf16[256,512]{1,0:T(8,128)(2,1)S(1)}, bf16[256,512]{1,0:T(8,128)(2,1)}, u32[]{:S(2)}) %copy-start.2) | copy-done | bytes 262168
  4.4 0.0 copy-start.3
  4.4 0.9 %copy-done.3 = bf16[256,256]{1,0:T(8,128)(2,1)S(1)} copy-done((bf16[256,256]{1,0:T(8,128)(2,1)S(1)}, bf16[256,256]{1,0:T(8,128)(2,1)}, u32[]{:S(2)}) %copy-start.3) | copy-done | bytes 131096
  5.3 0.0 copy-start.4
  5.3 0.9 %copy-done.4 = bf16[256,256]{1,0:T(8,128)(2,1)S(1)} copy-done((bf16[256,256]{1,0:T(8,128)(2,1)S(1)}, bf16[256,256]{1,0:T(8,128)(2,1)}, u32[]{:S(2)}) %copy-start.4) | copy-done | bytes 131096
  6.2 0.0 copy-start.5
  6.3 0.9 %copy-done.5 = bf16[256,256]{1,0:T(8,128)(2,1)S(1)} copy-done((bf16[256,256]{1,0:T(8,128)(2,1)S(1)}, bf16[256,256]{1,0:T(8,128)(2,1)}, u32[]{:S(2)}) %copy-start.5) | copy-done | bytes 131096
  7.2 0.0 copy-start.6
  7.2 0.9 %copy-done.6 = bf16[256,256]{1,0:T(8,128)(2,1)S(1)} copy-done((bf16[256,256]{1,0:T(8,128)(2,1)S(1)}, bf16[256,256]{1,0:T(8,128)(2,1)}, u32[]{:S(2)}) %copy-start.6) | copy-done | bytes 131096
  8.1 0.0 copy-start.7
  8.1 0.9 %copy-done.7 = bf16[256,256]{1,0:T(8,128)(2,1)S(1)} copy-done((bf16[256,256]{1,0:T(8,128)(2,1)S(1)}, bf16[256,256]{1,0:T(8,128)(2,1)}, u32[]{:S(2)}) %copy-start.7) | copy-done | bytes 131096
  9.0 0.0 copy-start.8
  9.0 0.9 %copy-done.8 = bf16[256,256]{1,0:T(8,128)(2,1)S(1)} copy-done((bf16[256,256]{1,0:T(8,128)(2,1)S(1)}, bf16[256,256]{1,0:T(8,128)(2,1)}, u32[]{:S(2)}) %copy-start.8) | copy-done | bytes 131096
  9.9 0.0 copy-start.9
  9.9 0.9 %copy-done.9 = bf16[256,256]{1,0:T(8,128)(2,1)S(1)} copy-done((bf16[256,256]{1,0:T(8,128)(2,1)S(1)}, bf16[256,256]{1,0:T(8,128)(2,1)}, u32[]{:S(2)}) %copy-start.9) | copy-done | bytes 131096
  10.8 0.0 copy-start.10
  10.8 0.8 %copy-done.10 = f32[128,128]{1,0:T(8,128)S(1)} copy-done((f32[128,128]{1,0:T(8,128)S(1)}, f32[128,128]{1,0:T(8,128)}, u32[]{:S(2)}) %copy-start.10) | copy-done | bytes 65560
  11.6 0.8 %copy-done.11 = f32[128,128]{1,0:T(8,128)S(1)} copy-done((f32[128,128]{1,0:T(8,128)S(1)}, f32[128,128]{1,0:T(8,128)}, u32[]{:S(2)}) %copy-start.11) | copy-done | bytes 65560
  12.5 0.8 %copy-done.12 = bf16[128,256]{1,0:T(8,128)(2,1)S(1)} copy-done((bf16[128,256]{1,0:T(8,128)(2,1)S(1)}, bf16[128,256]{1,0:T(8,128)(2,1)}, u32[]{:S(2)}) %copy-start.12) | copy-done | bytes 65560
  13.3 0.8 %copy-done.13 = bf16[128,256]{1,0:T(8,128)(2,1)S(1)} copy-done((bf16[128,256]{1,0:T(8,128)(2,1)S(1)}, bf16[128,256]{1,0:T(8,128)(2,1)}, u32[]{:S(2)}) %copy-start.13) | copy-done | bytes 65560
  14.1 57.1 %shard_map.174 = (bf16[256,512]{1,0:T(8,128)(2,1)S(1)}, f32[256,256]{1,0:T(8,128)S(1)}, f32[256,256]{1,0:T(8,128)S(1)}, f32[256,256]{1,0:T(8,128)S(1)}) custom-call(bf16[256,256]{1,0:T(8,128)(2,1)S(1)} %copy-done.3, bf16[256,256]{1,0:T(8,128)(2,1)S(1)} %copy-done.4, f32[256,256]{1,0:T(8,128)S(1)} %copy-done.1, f32[2,128]{1,0:T(2,128)S(1)} %bitcast.1, ...), custom_call_target="tpu_custom_call" | custom-call | tf_op jit(solution)/shard_map/pallas_call | solution.py:243
  71.2 0.7 copy.23
  71.9 0.7 copy.24
  72.6 0.7 copy.25
  73.3 0.7 copy.26
  (3 shorter events, 0.0 us)
Async XLA Ops:
  0.6 0.7 copy-start.14
  1.3 1.2 %copy-start = (bf16[1024,512]{1,0:T(8,128)(2,1)S(1)}, bf16[1024,512]{1,0:T(8,128)(2,1)}, u32[]{:S(2)}) copy-start(bf16[1024,512]{1,0:T(8,128)(2,1)} %weight_ref.1) | copy-start | bytes 3145732
  2.5 0.9 %copy-start.1 = (f32[256,256]{1,0:T(8,128)S(1)}, f32[256,256]{1,0:T(8,128)}, u32[]{:S(2)}) copy-start(f32[256,256]{1,0:T(8,128)} %taps_ref.1) | copy-start | bytes 786436
  3.5 0.9 %copy-start.2 = (bf16[256,512]{1,0:T(8,128)(2,1)S(1)}, bf16[256,512]{1,0:T(8,128)(2,1)}, u32[]{:S(2)}) copy-start(bf16[256,512]{1,0:T(8,128)(2,1)} %og_ref.1) | copy-start | bytes 786436
  4.4 0.9 %copy-start.3 = (bf16[256,256]{1,0:T(8,128)(2,1)S(1)}, bf16[256,256]{1,0:T(8,128)(2,1)}, u32[]{:S(2)}) copy-start(bf16[256,256]{1,0:T(8,128)(2,1)} %sig_ref.1) | copy-start | bytes 393220
  5.3 0.9 %copy-start.4 = (bf16[256,256]{1,0:T(8,128)(2,1)S(1)}, bf16[256,256]{1,0:T(8,128)(2,1)}, u32[]{:S(2)}) copy-start(bf16[256,256]{1,0:T(8,128)(2,1)} %gate_ref.1) | copy-start | bytes 393220
  6.2 0.9 %copy-start.5 = (bf16[256,256]{1,0:T(8,128)(2,1)S(1)}, bf16[256,256]{1,0:T(8,128)(2,1)}, u32[]{:S(2)}) copy-start(bf16[256,256]{1,0:T(8,128)(2,1)} %constant.24.clone.bckl_ref) | copy-start | bytes 393220
  7.2 0.9 %copy-start.6 = (bf16[256,256]{1,0:T(8,128)(2,1)S(1)}, bf16[256,256]{1,0:T(8,128)(2,1)}, u32[]{:S(2)}) copy-start(bf16[256,256]{1,0:T(8,128)(2,1)} %constant.23.clone.bckh_ref) | copy-start | bytes 393220
  8.1 0.9 %copy-start.7 = (bf16[256,256]{1,0:T(8,128)(2,1)S(1)}, bf16[256,256]{1,0:T(8,128)(2,1)}, u32[]{:S(2)}) copy-start(bf16[256,256]{1,0:T(8,128)(2,1)} %constant.22.clone.fwdl_ref) | copy-start | bytes 393220
  9.0 0.9 %copy-start.8 = (bf16[256,256]{1,0:T(8,128)(2,1)S(1)}, bf16[256,256]{1,0:T(8,128)(2,1)}, u32[]{:S(2)}) copy-start(bf16[256,256]{1,0:T(8,128)(2,1)} %constant.21.clone.fwdh_ref) | copy-start | bytes 393220
  9.9 0.9 %copy-start.9 = (bf16[256,256]{1,0:T(8,128)(2,1)S(1)}, bf16[256,256]{1,0:T(8,128)(2,1)}, u32[]{:S(2)}) copy-start(bf16[256,256]{1,0:T(8,128)(2,1)} %constant.18.clone.first_ref) | copy-start | bytes 393220
  10.8 0.8 %copy-start.10 = (f32[128,128]{1,0:T(8,128)S(1)}, f32[128,128]{1,0:T(8,128)}, u32[]{:S(2)}) copy-start(f32[128,128]{1,0:T(8,128)} %constant.26.clone.sin_ref) | copy-start | bytes 196612
  11.6 0.8 %copy-start.11 = (f32[128,128]{1,0:T(8,128)S(1)}, f32[128,128]{1,0:T(8,128)}, u32[]{:S(2)}) copy-start(f32[128,128]{1,0:T(8,128)} %constant.25.clone.cos_ref) | copy-start | bytes 196612
  12.5 0.8 %copy-start.12 = (bf16[128,256]{1,0:T(8,128)(2,1)S(1)}, bf16[128,256]{1,0:T(8,128)(2,1)}, u32[]{:S(2)}) copy-start(bf16[128,256]{1,0:T(8,128)(2,1)} %constant.20.clone.lastl_ref) | copy-start | bytes 196612
  13.3 0.8 %copy-start.13 = (bf16[128,256]{1,0:T(8,128)(2,1)S(1)}, bf16[128,256]{1,0:T(8,128)(2,1)}, u32[]{:S(2)}) copy-start(bf16[128,256]{1,0:T(8,128)(2,1)} %constant.19.clone.lasth_ref) | copy-start | bytes 196612
where the time goes:
time: 74.6 us; the launch traced here: 74 us
  Pallas kernels  57.1 us (77%)
  local copies, waits for them, and re-layouts  16.3 us (22%)
    pallas_call x1, Pallas kernels, per_device(): pl.pallas_call(functools.partial(body, shards, chans), out_shape=(jax.Sha...  57.1 us
    unnamed x34, local copies, waits for them, and re-layouts  16.3 us

commit v1 on v0

--- a/solution.py
+++ b/solution.py
@@ -35,13 +35,9 @@
     first_high, first_low = halves(first)
     last_high, last_low = halves(first.T / length)
     return (
-        np.concatenate([first_high, first_low], 1),
-        last_high,
-        last_low,
-        *halves(ahead),
-        *halves(back),
-        np.cos(turn).astype(np.float32),
-        (-np.sin(turn)).astype(np.float32),
+        np.stack([np.concatenate([first_high, first_low], 1), *halves(ahead), *halves(back)]),
+        np.stack([last_high, last_low]),
+        np.stack([np.cos(turn), -np.sin(turn)]).astype(np.float32),
     )
 
 
@@ -56,12 +52,12 @@
 
 def body(
     shards, chans,
-    sig_ref, gate_ref, taps_ref, decay_ref, weight_ref, og_ref,
-    first_ref, lasth_ref, lastl_ref, fwdh_ref, fwdl_ref, bckh_ref, bckl_ref, cos_ref, sin_ref,
+    sig_hbm, gate_hbm, taps_hbm, decay_hbm, weight_hbm, og_hbm, square_hbm, last_hbm, turn_hbm,
     out_ref, sgrad_ref, ggrad_ref, tgrad_ref,
     in_send, in_recv, rs_send, rs_recv, mx_send, mx_recv, gr_send, gr_recv, rt_send, rt_recv, ag_send, ag_recv,
     rows, window, grad_out, xcat, bh, bl, spec, zh, zl,
-    sends, recvs,
+    sig_ref, gate_ref, taps_ref, decay_ref, weight_ref, og_ref, square_ref, last_ref, turn_ref,
+    sends, recvs, loads,
 ):
     me, ch = lax.axis_index("seq"), lax.axis_index("chan")
     far = lax.rem(ch + chans // 2, chans)
@@ -69,6 +65,20 @@
     folds = span // LANES
     mine = wide // shards
     n1 = shards * folds
+
+    arrivals = [
+        pltpu.make_async_copy(source, target, loads.at[k])
+        for k, (source, target) in enumerate(
+            (
+                (sig_hbm, sig_ref), (taps_hbm, taps_ref), (og_hbm, og_ref), (weight_hbm, weight_ref),
+                (square_hbm, square_ref), (last_hbm, last_ref), (turn_hbm, turn_ref), (gate_hbm, gate_ref), (decay_hbm, decay_ref),
+            )
+        )
+    ]
+    for k in (8, 0, 1, 2, 3, 4, 5, 6, 7):
+        arrivals[k].start()
+    first_ref, fwdh_ref, fwdl_ref, bckh_ref, bckl_ref = (square_ref.at[k] for k in range(5))
+    lasth_ref, lastl_ref = last_ref.at[0], last_ref.at[1]
 
     barrier = pltpu.get_barrier_semaphore()
 
@@ -103,6 +113,7 @@
             source, target, sends.at[k], recvs.at[k], device_id=(me, far), device_id_type=MESH
         )
 
+    arrivals[8].wait()
     place = lax.broadcasted_iota(jnp.int32, (1, span), 1) + me * span
     place = place.astype(F32)
     for i in range(wide // LANES):
@@ -113,11 +124,16 @@
             cols = slice(h * LANES, (h + 1) * LANES)
             window[i * LANES : (i + 1) * LANES, cols] = jnp.exp(-rate * place[:, cols]) * size
 
+    arrivals[0].wait()
+    arrivals[1].wait()
     in_send[:, 0] = to_rows(sig_ref[...].astype(F32))
     in_send[:, 1] = to_rows(taps_ref[...] * window[...])
 
     pl.semaphore_wait(barrier, shards + len(near))
     spread(in_send, in_recv, 0)
+
+    arrivals[2].wait()
+    arrivals[3].wait()
 
     def share(k):
         block = lax.rem(ch + k, chans)
@@ -132,7 +148,9 @@
         ).start()
     grad_out[...] = share(0).astype(BF16).astype(F32)
 
-    cosine, sine = cos_ref[...], sin_ref[...]
+    for arrival in arrivals[4:8]:
+        arrival.wait()
+    cosine, sine = turn_ref[0], turn_ref[1]
 
     def analyse(block, base):
         rows[...] = block.astype(F32).reshape(wide * folds, LANES)
@@ -233,6 +251,29 @@
     joint(rt_send, rt_recv, 5).wait_send()
 
 
+def store(*refs):
+    half = len(refs) // 2
+    copies = [
+        pltpu.make_async_copy(refs[k], refs[half + k], refs[-1].at[k]) for k in range(half)
+    ]
+    for copy in copies:
+        copy.start()
+    for copy in copies:
+        copy.wait()
+
+
+def stored(values):
+    away = pl.BlockSpec(memory_space=pl.ANY)
+    return pl.pallas_call(
+        store,
+        out_shape=tuple(jax.ShapeDtypeStruct(x.shape, x.dtype) for x in values),
+        in_specs=[away] * len(values),
+        out_specs=(pl.BlockSpec(memory_space=pltpu.HBM),) * len(values),
+        scratch_shapes=[pltpu.SemaphoreType.DMA((len(values),))],
+        compiler_params=pltpu.CompilerParams(vmem_limit_bytes=1 << 20),
+    )(*values)
+
+
 def per_device(shards, chans, consts, signal, gating, filter_taps, decay_rates, out_weight, out_grad):
     wide, span = signal.shape
     folds = span // LANES
@@ -240,7 +281,8 @@
     n1 = shards * folds
     tile = (mine * folds, LANES)
     vmem = pl.BlockSpec(memory_space=pltpu.VMEM)
-    return pl.pallas_call(
+    away = pl.BlockSpec(memory_space=pltpu.HBM)
+    results = pl.pallas_call(
         functools.partial(body, shards, chans),
         out_shape=(
             jax.ShapeDtypeStruct(out_grad.shape, BF16),
@@ -248,7 +290,7 @@
             jax.ShapeDtypeStruct(signal.shape, F32),
             jax.ShapeDtypeStruct(signal.shape, F32),
         ),
-        in_specs=[vmem] * (6 + len(consts)),
+        in_specs=[away] * (6 + len(consts)),
         out_specs=(vmem,) * 4,
         scratch_shapes=[
             pltpu.VMEM((shards, 2, *tile), BF16),
@@ -272,13 +314,22 @@
             pltpu.VMEM((3, mine * n1, 2 * LANES), F32),
             pltpu.VMEM((2 * n1, mine * LANES), BF16),
             pltpu.VMEM((2 * n1, mine * LANES), BF16),
+            *(pltpu.VMEM(x.shape, x.dtype) for x in (signal, gating, filter_taps)),
+            pltpu.VMEM((wide // LANES, LANES), F32),
+            *(pltpu.VMEM(x.shape, x.dtype) for x in (out_weight, out_grad, *consts)),
             pltpu.SemaphoreType.DMA((6,)),
             pltpu.SemaphoreType.DMA((6,)),
+            pltpu.SemaphoreType.DMA((9,)),
         ],
-        compiler_params=pltpu.CompilerParams(collective_id=0, has_side_effects=True, vmem_limit_bytes=48 << 20),
+        compiler_params=pltpu.CompilerParams(collective_id=0, has_side_effects=True, vmem_limit_bytes=24 << 20),
     )(
-        signal, gating, filter_taps, decay_rates.reshape(-1, LANES), out_weight, out_grad, *map(jnp.asarray, consts)
+        *(
+            pltpu.with_memory_space_constraint(x, pltpu.HBM)
+            for x in (signal, gating, filter_taps, decay_rates.reshape(-1, LANES), out_weight, out_grad)
+        ),
+        *(pltpu.with_memory_space_constraint(jnp.asarray(x), pltpu.HBM) for x in consts),
     )
+    return stored(results)
 
 
 def solution(mesh):

time: 74.6 us -> 59.2 us (0.79)
  local copies, waits for them, and re-layouts: 16.3 us -> 0 us
  Pallas kernels: 57.1 us -> 58.4 us
    unnamed x34 -> x0, local copies, waits for them, and re-layouts: 16.3 us -> none
    pallas_call x0 -> x1, Pallas kernels: none -> 1 us  [stored(): pl.pallas_call(store, out_shape=tuple((jax.ShapeDtypeStruct(x.shape, x.dt...]
where the time goes in v1:
time: 59.2 us; the launch traced here: 59.1 us
  Pallas kernels  58.4 us (99%)
  between operations  0.64 us (1%)
    pallas_call x1, Pallas kernels, per_device(): pl.pallas_call(functools.partial(body, shards, chans), out_shape=(jax.Sha...  57.4 us

profile of v1, /device:TPU:1, one launch (start us, length us, event | category | flops | bytes accessed | tf_op | source)
XLA Modules:
  0.0 59.1 jit_solution(2190662945596195163)
XLA Ops:
  0.6 57.4 %shard_map.120 = (bf16[256,512]{1,0:T(8,128)(2,1)S(1)}, f32[256,256]{1,0:T(8,128)S(1)}, f32[256,256]{1,0:T(8,128)S(1)}, f32[256,256]{1,0:T(8,128)S(1)}) custom-call(bf16[256,256]{1,0:T(8,128)(2,1)} %sig_hbm.1, bf16[256,256]{1,0:T(8,128)(2,1)} %gate_hbm.1, f32[256,256]{1,0:T(8,128)} %taps_hbm.1, f32[2,128]{1,0:T(2,128)} %bitcast.1, ...), custom_call_target="tpu_custom_call" | custom-call | tf_op jit(solution)/shard_map/pallas_call | solution.py:285
  58.1 1.0 %shard_map.121 = (bf16[256,512]{1,0:T(8,128)(2,1)}, f32[256,256]{1,0:T(8,128)}, f32[256,256]{1,0:T(8,128)}, f32[256,256]{1,0:T(8,128)}) custom-call(bf16[256,512]{1,0:T(8,128)(2,1)S(1)} %get-tuple-element.8.refs_0_, f32[256,256]{1,0:T(8,128)S(1)} %get-tuple-element.9.refs_1_, f32[256,256]{1,0:T(8,128)S(1)} %get-tuple-element.10.refs_2_, ...), custom_call_target="tpu_custom_call" | custom-call | tf_op jit(solution)/shard_map/pallas_call | solution.py:267

commit v2 on v1

--- a/solution.py
+++ b/solution.py
@@ -55,12 +55,19 @@
     sig_hbm, gate_hbm, taps_hbm, decay_hbm, weight_hbm, og_hbm, square_hbm, last_hbm, turn_hbm,
     out_ref, sgrad_ref, ggrad_ref, tgrad_ref,
     in_send, in_recv, rs_send, rs_recv, mx_send, mx_recv, gr_send, gr_recv, rt_send, rt_recv, ag_send, ag_recv,
+    rs_relay, partial,
     rows, window, grad_out, xcat, bh, bl, spec, zh, zl,
     sig_ref, gate_ref, taps_ref, decay_ref, weight_ref, og_ref, square_ref, last_ref, turn_ref,
-    sends, recvs, loads,
+    sends, recvs, loads, come, go,
 ):
     me, ch = lax.axis_index("seq"), lax.axis_index("chan")
     far = lax.rem(ch + chans // 2, chans)
+    mate = ch + 1 - 2 * lax.rem(ch, 2)
+    opposite = chans - 1 - ch
+    low = ch < chans // 2
+    inner = jnp.logical_or(ch == 1, ch == 2)
+    centre = jnp.where(low, 2, 1)
+    edge = jnp.where(low, chans - 1, 0)
     wide, span = sig_ref.shape
     folds = span // LANES
     mine = wide // shards
@@ -75,20 +82,30 @@
             )
         )
     ]
-    for k in (8, 0, 1, 2, 3, 4, 5, 6, 7):
+    for k in (2, 3, 8, 0, 1, 4, 5, 6, 7):
         arrivals[k].start()
     first_ref, fwdh_ref, fwdl_ref, bckh_ref, bckl_ref = (square_ref.at[k] for k in range(5))
     lasth_ref, lastl_ref = last_ref.at[0], last_ref.at[1]
 
     barrier = pltpu.get_barrier_semaphore()
 
-    @pl.loop(0, shards)
-    def _(i):
-        pl.semaphore_signal(barrier, inc=1, device_id=(i, far), device_id_type=MESH)
-
-    near = [k for k in range(1, chans) if k != chans // 2]
-    for k in near:
-        pl.semaphore_signal(barrier, inc=1, device_id=(me, lax.rem(ch + k, chans)), device_id_type=MESH)
+    def tell(semaphore, seq, chan):
+        pl.semaphore_signal(semaphore, inc=1, device_id=(seq, chan), device_id_type=MESH)
+
+    lead = ch == 0
+
+    @pl.when(lead)
+    def _():
+        for k in range(1, chans):
+            tell(barrier, me, k)
+
+    @pl.when(jnp.logical_not(lead))
+    def _():
+        for k in range(1, chans):
+
+            @pl.when(ch != k)
+            def _():
+                tell(barrier, me, k)
 
     def to_rows(value):
         for h in range(folds):
@@ -112,6 +129,57 @@
         return pltpu.make_async_remote_copy(
             source, target, sends.at[k], recvs.at[k], device_id=(me, far), device_id_type=MESH
         )
+
+    arrivals[2].wait()
+    arrivals[3].wait()
+
+    def share(block):
+        part = weight_ref[pl.ds(pl.multiple_of(block * wide, wide), wide), :]
+        return lax.dot_general(part, og_ref[...], (((1,), (1,)), ((), ())), preferred_element_type=F32)
+
+    def along(source, target, k, to):
+        return pltpu.make_async_remote_copy(
+            source, target, sends.at[k], recvs.at[k], device_id=(me, to), device_id_type=MESH
+        )
+
+    half = wide // 2
+    cuts = [pl.ds(h * half, half) for h in range(2)]
+    relayed = share(edge)
+
+    @pl.when(jnp.logical_not(lead))
+    def _():
+        pl.semaphore_wait(barrier, chans - 1)
+        tell(come, me, 0)
+
+    @pl.when(lead)
+    def _():
+        pl.semaphore_wait(come, chans - 1)
+
+        @pl.loop(1, shards)
+        def _(i):
+            tell(barrier, lax.rem(me + i, shards), 0)
+
+    @pl.when(jnp.logical_not(inner))
+    def _():
+        rs_send[2] = relayed.astype(BF16)
+        for h, cut in enumerate(cuts):
+            along(rs_send.at[2, cut], rs_relay.at[cut], 6 + h, mate).start()
+
+    @pl.when(inner)
+    def _():
+        partial[...] = relayed
+
+    rs_send[0] = share(mate).astype(BF16)
+    along(rs_send.at[0], rs_recv.at[0], 8, mate).start()
+    rs_send[1] = share(centre).astype(BF16)
+
+    @pl.when(inner)
+    def _():
+        along(rs_send.at[1], rs_recv.at[2], 10, centre).start()
+
+    @pl.when(jnp.logical_not(inner))
+    def _():
+        along(rs_send.at[1], rs_recv.at[1], 9, centre).start()
 
     arrivals[8].wait()
     place = lax.broadcasted_iota(jnp.int32, (1, span), 1) + me * span
@@ -129,24 +197,26 @@
     in_send[:, 0] = to_rows(sig_ref[...].astype(F32))
     in_send[:, 1] = to_rows(taps_ref[...] * window[...])
 
-    pl.semaphore_wait(barrier, shards + len(near))
+    @pl.when(inner)
+    def _():
+        for h, cut in enumerate(cuts):
+            along(rs_send.at[2, cut], rs_relay.at[cut], 6 + h, mate).wait_recv()
+            rs_send[2, cut] = (partial[cut, :] + rs_relay[cut, :].astype(F32)).astype(BF16)
+            along(rs_send.at[2, cut], rs_recv.at[1, cut], 9, edge).start()
+
+    @pl.when(lead)
+    def _():
+        pl.semaphore_wait(barrier, shards - 1)
+        for k in range(1, chans):
+            tell(go, me, k)
+
+    @pl.when(jnp.logical_not(lead))
+    def _():
+        pl.semaphore_wait(go, 1)
+
     spread(in_send, in_recv, 0)
 
-    arrivals[2].wait()
-    arrivals[3].wait()
-
-    def share(k):
-        block = lax.rem(ch + k, chans)
-        part = weight_ref[pl.ds(pl.multiple_of(block * wide, wide), wide), :]
-        return lax.dot_general(part, og_ref[...], (((1,), (1,)), ((), ())), preferred_element_type=F32)
-
-    for k in range(1, chans):
-        rs_send[k - 1] = share(k).astype(BF16)
-        pltpu.make_async_remote_copy(
-            rs_send.at[k - 1], rs_recv.at[k - 1], sends.at[1], recvs.at[1],
-            device_id=(me, lax.rem(ch + k, chans)), device_id_type=MESH,
-        ).start()
-    grad_out[...] = share(0).astype(BF16).astype(F32)
+    grad_out[...] = share(ch).astype(BF16).astype(F32)
 
     for arrival in arrivals[4:8]:
         arrival.wait()
@@ -191,6 +261,19 @@
     def parts(k):
         return spec[k, :, :LANES], spec[k, :, LANES:]
 
+    along(rs_send.at[0], rs_recv.at[0], 8, mate).wait_recv()
+    along(rs_send.at[1], rs_recv.at[1], 9, mate).wait_recv()
+    grad_out[...] = grad_out[...] + rs_recv[0].astype(F32) + rs_recv[1].astype(F32)
+
+    @pl.when(inner)
+    def _():
+        along(rs_send.at[1], rs_recv.at[2], 10, mate).wait_recv()
+        grad_out[...] = grad_out[...] + rs_recv[2].astype(F32)
+
+    total = grad_out[...]
+    gr_send[...] = to_rows(total * gate_ref[...].astype(F32))
+    spread(gr_send, gr_recv, 3)
+
     joint(in_send, in_recv, 0).wait_recv()
     analyse(in_recv[:, 0], 0)
     analyse(in_recv[:, 1], 1)
@@ -198,57 +281,91 @@
     mx_send[...] = synthesize(sr * fr - si * fi, sr * fi + si * fr)
     spread(mx_send, mx_recv, 2)
 
-    joint(rs_send, rs_recv, 1).wait_recv()
-    total = grad_out[...]
-    for k in range(chans - 1):
-        total = total + rs_recv[k].astype(F32)
-    grad_out[...] = total
-    gr_send[...] = to_rows(total * gate_ref[...].astype(F32))
-    spread(gr_send, gr_recv, 3)
-
-    joint(mx_send, mx_recv, 2).wait_recv()
-    mixed = jnp.concatenate(from_rows(mx_recv[...]), 1)
-    ag_send[...] = jnp.transpose(mixed * gate_ref[...].astype(F32)).astype(BF16)
-    for k in range(1, chans):
-        pltpu.make_async_remote_copy(
-            ag_send, ag_recv.at[k - 1], sends.at[4], recvs.at[4],
-            device_id=(me, lax.rem(ch + k, chans)), device_id_type=MESH,
-        ).start()
-    ggrad_ref[...] = grad_out[...] * mixed
-
     joint(gr_send, gr_recv, 3).wait_recv()
     analyse(gr_recv[...], 2)
     gr, gi = parts(2)
     fr, fi = parts(1)
-    rt_send[:, 0] = synthesize(gr * fr + gi * fi, gi * fr - gr * fi)
+    rt_send[0] = synthesize(gr * fr + gi * fi, gi * fr - gr * fi)
+    spread(rt_send.at[0], rt_recv.at[0], 5)
     sr, si = parts(0)
     gr, gi = parts(2)
-    rt_send[:, 1] = synthesize(gr * sr + gi * si, gi * sr - gr * si)
-    spread(rt_send, rt_recv, 5)
+    rt_send[1] = synthesize(gr * sr + gi * si, gi * sr - gr * si)
+    spread(rt_send.at[1], rt_recv.at[1], 4)
+
+    joint(mx_send, mx_recv, 2).wait_recv()
+    mixed = jnp.concatenate(from_rows(mx_recv[...]), 1)
+    ag_send[...] = jnp.transpose(mixed * gate_ref[...].astype(F32)).astype(BF16)
+    for h, cut in enumerate(cuts):
+        along(ag_send.at[cut], ag_recv.at[1, cut], 11 + h, far).start()
+
+    @pl.when(inner)
+    def _():
+        along(ag_send, ag_recv.at[2], 14, opposite).start()
+
+    along(ag_send, ag_recv.at[0], 13, mate).start()
+    ggrad_ref[...] = grad_out[...] * mixed
+
+    for h, cut in enumerate(cuts):
+        along(ag_send.at[cut], ag_recv.at[1, cut], 11 + h, far).wait_recv()
+
+        @pl.when(inner)
+        def _():
+            along(ag_recv.at[1, cut], ag_recv.at[2, cut], 15, mate).start()
 
     def project(block, gathered):
         part = weight_ref[pl.ds(pl.multiple_of(block * wide, wide), wide), :]
         return mm(gathered, part)
 
-    joint(ag_recv, ag_recv, 4).wait_recv()
-    total = project(ch, ag_send[...])
-    for k in range(1, chans):
-        total = total + project(lax.rem(ch + chans - k, chans), ag_recv[k - 1])
+    total = project(ch, ag_send[...]) + project(far, ag_recv[1])
+    along(ag_send, ag_recv.at[0], 13, mate).wait_recv()
+    total = total + project(mate, ag_recv[0])
+
+    @pl.when(inner)
+    def _():
+        along(ag_send, ag_recv.at[2], 14, opposite).wait_recv()
+
+    @pl.when(jnp.logical_not(inner))
+    def _():
+        along(ag_send, ag_recv.at[2], 15, mate).wait_recv()
+
+    total = total + project(opposite, ag_recv[2])
     out_ref[...] = total.astype(BF16)
 
-    joint(rt_send, rt_recv, 5).wait_recv()
-    for h, value in enumerate(from_rows(rt_recv[:, 0])):
+    joint(rt_send.at[0], rt_recv.at[0], 5).wait_recv()
+    for h, value in enumerate(from_rows(rt_recv[0])):
         sgrad_ref[:, h * LANES : (h + 1) * LANES] = value
-    for h, value in enumerate(from_rows(rt_recv[:, 1])):
+    joint(rt_send.at[1], rt_recv.at[1], 4).wait_recv()
+    for h, value in enumerate(from_rows(rt_recv[1])):
         cols = slice(h * LANES, (h + 1) * LANES)
         tgrad_ref[:, cols] = value * window[:, cols]
 
     joint(in_send, in_recv, 0).wait_send()
-    joint(rs_send, rs_recv, 1).wait_send()
+    along(rs_send.at[0], rs_recv.at[0], 8, mate).wait_send()
+
+    @pl.when(inner)
+    def _():
+        along(rs_send.at[1], rs_recv.at[2], 10, mate).wait_send()
+        along(rs_send.at[2], rs_recv.at[1], 9, mate).wait_send()
+
+    @pl.when(jnp.logical_not(inner))
+    def _():
+        along(rs_send.at[1], rs_recv.at[1], 9, mate).wait_send()
+        for h, cut in enumerate(cuts):
+            along(rs_send.at[2, cut], rs_relay.at[cut], 6 + h, mate).wait_send()
+
     joint(mx_send, mx_recv, 2).wait_send()
     joint(gr_send, gr_recv, 3).wait_send()
-    joint(ag_recv, ag_recv, 4).wait_send()
-    joint(rt_send, rt_recv, 5).wait_send()
+    for h, cut in enumerate(cuts):
+        along(ag_send.at[cut], ag_recv.at[1, cut], 11 + h, far).wait_send()
+    along(ag_send, ag_recv.at[0], 13, mate).wait_send()
+
+    @pl.when(inner)
+    def _():
+        along(ag_send, ag_recv.at[2], 14, mate).wait_send()
+        along(ag_recv.at[1], ag_recv.at[2], 15, mate).wait_send()
+
+    joint(rt_send.at[0], rt_recv.at[0], 5).wait_send()
+    joint(rt_send.at[1], rt_recv.at[1], 4).wait_send()
 
 
 def store(*refs):
@@ -301,10 +418,12 @@
             pltpu.VMEM((shards, *tile), BF16),
             pltpu.VMEM((shards, *tile), BF16),
             pltpu.VMEM((shards, *tile), BF16),
-            pltpu.VMEM((shards, 2, *tile), BF16),
-            pltpu.VMEM((shards, 2, *tile), BF16),
+            pltpu.VMEM((2, shards, *tile), BF16),
+            pltpu.VMEM((2, shards, *tile), BF16),
             pltpu.VMEM((span, wide), BF16),
             pltpu.VMEM((chans - 1, span, wide), BF16),
+            pltpu.VMEM((wide, span), BF16),
+            pltpu.VMEM((wide, span), F32),
             pltpu.VMEM((wide * folds, LANES), F32),
             pltpu.VMEM((wide, span), F32),
             pltpu.VMEM((wide, span), F32),
@@ -317,9 +436,11 @@
             *(pltpu.VMEM(x.shape, x.dtype) for x in (signal, gating, filter_taps)),
             pltpu.VMEM((wide // LANES, LANES), F32),
             *(pltpu.VMEM(x.shape, x.dtype) for x in (out_weight, out_grad, *consts)),
-            pltpu.SemaphoreType.DMA((6,)),
-            pltpu.SemaphoreType.DMA((6,)),
+            pltpu.SemaphoreType.DMA((16,)),
+            pltpu.SemaphoreType.DMA((16,)),
             pltpu.SemaphoreType.DMA((9,)),
+            pltpu.SemaphoreType.REGULAR,
+            pltpu.SemaphoreType.REGULAR,
         ],
         compiler_params=pltpu.CompilerParams(collective_id=0, has_side_effects=True, vmem_limit_bytes=24 << 20),
     )(

time: 59.2 us -> 55.2 us (0.932)
  Pallas kernels: 58.4 us -> 54.4 us
    pallas_call x1, Pallas kernels: 57.4 us -> 53.4 us  [per_device(): pl.pallas_call(functools.partial(body, shards, chans), out_shape=(jax.Sha...]
where the time goes in v2:
time: 55.2 us; the launch traced here: 55.1 us
  Pallas kernels  54.4 us (99%)
  between operations  0.64 us (1%)
    pallas_call x1, Pallas kernels, per_device(): pl.pallas_call(functools.partial(body, shards, chans), out_shape=(jax.Sha...  53.4 us

profile of v2, /device:TPU:1, one launch (start us, length us, event | category | flops | bytes accessed | tf_op | source)
XLA Modules:
  0.0 55.1 jit_solution(7838261266953008174)
XLA Ops:
  0.6 53.4 %shard_map.120 = (bf16[256,512]{1,0:T(8,128)(2,1)S(1)}, f32[256,256]{1,0:T(8,128)S(1)}, f32[256,256]{1,0:T(8,128)S(1)}, f32[256,256]{1,0:T(8,128)S(1)}) custom-call(bf16[256,256]{1,0:T(8,128)(2,1)} %sig_hbm.1, bf16[256,256]{1,0:T(8,128)(2,1)} %gate_hbm.1, f32[256,256]{1,0:T(8,128)} %taps_hbm.1, f32[2,128]{1,0:T(2,128)} %bitcast.1, ...), custom_call_target="tpu_custom_call" | custom-call | tf_op jit(solution)/shard_map/pallas_call | solution.py:402
  54.1 1.0 %shard_map.121 = (bf16[256,512]{1,0:T(8,128)(2,1)}, f32[256,256]{1,0:T(8,128)}, f32[256,256]{1,0:T(8,128)}, f32[256,256]{1,0:T(8,128)}) custom-call(bf16[256,512]{1,0:T(8,128)(2,1)S(1)} %get-tuple-element.8.refs_0_, f32[256,256]{1,0:T(8,128)S(1)} %get-tuple-element.9.refs_1_, f32[256,256]{1,0:T(8,128)S(1)} %get-tuple-element.10.refs_2_, ...), custom_call_target="tpu_custom_call" | custom-call | tf_op jit(solution)/shard_map/pallas_call | solution.py:384

commit v3 on v2

--- a/solution.py
+++ b/solution.py
@@ -92,16 +92,17 @@
     def tell(semaphore, seq, chan):
         pl.semaphore_signal(semaphore, inc=1, device_id=(seq, chan), device_id_type=MESH)
 
-    lead = ch == 0
+    lead = ch == 1
+    others = [k for k in range(chans) if k != 1]
 
     @pl.when(lead)
     def _():
-        for k in range(1, chans):
+        for k in others:
             tell(barrier, me, k)
 
     @pl.when(jnp.logical_not(lead))
     def _():
-        for k in range(1, chans):
+        for k in others:
 
             @pl.when(ch != k)
             def _():
@@ -149,7 +150,7 @@
     @pl.when(jnp.logical_not(lead))
     def _():
         pl.semaphore_wait(barrier, chans - 1)
-        tell(come, me, 0)
+        tell(come, me, 1)
 
     @pl.when(lead)
     def _():
@@ -157,7 +158,7 @@
 
         @pl.loop(1, shards)
         def _(i):
-            tell(barrier, lax.rem(me + i, shards), 0)
+            tell(barrier, lax.rem(me + i, shards), 1)
 
     @pl.when(jnp.logical_not(inner))
     def _():
@@ -207,7 +208,7 @@
     @pl.when(lead)
     def _():
         pl.semaphore_wait(barrier, shards - 1)
-        for k in range(1, chans):
+        for k in others:
             tell(go, me, k)
 
     @pl.when(jnp.logical_not(lead))
@@ -272,6 +273,7 @@
 
     total = grad_out[...]
     gr_send[...] = to_rows(total * gate_ref[...].astype(F32))
+    joint(in_send, in_recv, 0).wait_send()
     spread(gr_send, gr_recv, 3)
 
     joint(in_send, in_recv, 0).wait_recv()
@@ -339,7 +341,6 @@
         cols = slice(h * LANES, (h + 1) * LANES)
         tgrad_ref[:, cols] = value * window[:, cols]
 
-    joint(in_send, in_recv, 0).wait_send()
     along(rs_send.at[0], rs_recv.at[0], 8, mate).wait_send()
 
     @pl.when(inner)

time: 55.2 us -> 53.7 us (0.973)
  Pallas kernels: 54.4 us -> 53 us
    pallas_call x1, Pallas kernels: 53.4 us -> 52 us  [per_device(): pl.pallas_call(functools.partial(body, shards, chans), out_shape=(jax.Sha...]
where the time goes in v3:
time: 53.7 us; the launch traced here: 53.6 us
  Pallas kernels  53 us (99%)
  between operations  0.64 us (1%)
    pallas_call x1, Pallas kernels, per_device(): pl.pallas_call(functools.partial(body, shards, chans), out_shape=(jax.Sha...  52 us

profile of v3, /device:TPU:1, one launch (start us, length us, event | category | flops | bytes accessed | tf_op | source)
XLA Modules:
  0.0 53.6 jit_solution(6536991684006158063)
XLA Ops:
  0.6 52.0 %shard_map.120 = (bf16[256,512]{1,0:T(8,128)(2,1)S(1)}, f32[256,256]{1,0:T(8,128)S(1)}, f32[256,256]{1,0:T(8,128)S(1)}, f32[256,256]{1,0:T(8,128)S(1)}) custom-call(bf16[256,256]{1,0:T(8,128)(2,1)} %sig_hbm.1, bf16[256,256]{1,0:T(8,128)(2,1)} %gate_hbm.1, f32[256,256]{1,0:T(8,128)} %taps_hbm.1, f32[2,128]{1,0:T(2,128)} %bitcast.1, ...), custom_call_target="tpu_custom_call" | custom-call | tf_op jit(solution)/shard_map/pallas_call | solution.py:403
  52.6 1.0 %shard_map.121 = (bf16[256,512]{1,0:T(8,128)(2,1)}, f32[256,256]{1,0:T(8,128)}, f32[256,256]{1,0:T(8,128)}, f32[256,256]{1,0:T(8,128)}) custom-call(bf16[256,512]{1,0:T(8,128)(2,1)S(1)} %get-tuple-element.8.refs_0_, f32[256,256]{1,0:T(8,128)S(1)} %get-tuple-element.9.refs_1_, f32[256,256]{1,0:T(8,128)S(1)} %get-tuple-element.10.refs_2_, ...), custom_call_target="tpu_custom_call" | custom-call | tf_op jit(solution)/shard_map/pallas_call | solution.py:385

commit v4 on v3

--- a/solution.py
+++ b/solution.py
@@ -108,14 +108,22 @@
             def _():
                 tell(barrier, me, k)
 
-    def to_rows(value):
-        for h in range(folds):
-            rows[pl.ds(h, wide, stride=folds), :] = value[:, h * LANES : (h + 1) * LANES]
+    group = wide // 2
+    pair = mine // 2
+
+    def piece(g, h):
+        return slice(g * group, (g + 1) * group), slice(h * LANES, (h + 1) * LANES)
+
+    def to_rows(pieces):
+        for k, value in enumerate(pieces):
+            rows[pl.ds(k, group, stride=2 * folds), :] = value
         return rows[...].reshape(shards, mine * folds, LANES).astype(BF16)
 
     def from_rows(block):
         rows[...] = block.astype(F32).reshape(wide * folds, LANES)
-        return [rows[pl.ds(h, wide, stride=folds), :] for h in range(folds)]
+        return [
+            (piece(g, h), rows[pl.ds(g * folds + h, group, stride=2 * folds), :]) for g in range(2) for h in range(folds)
+        ]
 
     def spread(source, target, k):
         @pl.loop(0, shards)
@@ -195,8 +203,11 @@
 
     arrivals[0].wait()
     arrivals[1].wait()
-    in_send[:, 0] = to_rows(sig_ref[...].astype(F32))
-    in_send[:, 1] = to_rows(taps_ref[...] * window[...])
+    for g in range(2):
+        spots = [piece(g, h) for h in range(folds)]
+        in_send[g] = to_rows(
+            [sig_ref[spot].astype(F32) for spot in spots] + [taps_ref[spot] * window[spot] for spot in spots]
+        )
 
     @pl.when(inner)
     def _():
@@ -215,7 +226,8 @@
     def _():
         pl.semaphore_wait(go, 1)
 
-    spread(in_send, in_recv, 0)
+    spread(in_send.at[0], in_recv.at[0], 0)
+    spread(in_send.at[1], in_recv.at[1], 1)
 
     grad_out[...] = share(ch).astype(BF16).astype(F32)
 
@@ -225,42 +237,64 @@
 
     def analyse(block, base):
         rows[...] = block.astype(F32).reshape(wide * folds, LANES)
-        for c in range(mine):
+        for k in range(mine):
+            start = (k % pair) * 2 * folds + (k // pair) * folds
             column = jnp.concatenate(
-                [rows[pl.ds(c * folds + h, shards, stride=mine * folds), :] for h in range(folds)], 0
+                [rows[pl.ds(start + h, shards, stride=mine * folds), :] for h in range(folds)], 0
             ).astype(BF16)
-            cols = slice(c * LANES, (c + 1) * LANES)
+            cols = slice(k * LANES, (k + 1) * LANES)
             xcat[:n1, cols] = column
             xcat[n1:, cols] = column
         stage = mm(first_ref[...], xcat[...])
-        for c in range(mine):
-            cols = slice(c * LANES, (c + 1) * LANES)
+        for k in range(mine):
+            cols = slice(k * LANES, (k + 1) * LANES)
             real, imag = stage[:n1, cols], stage[n1:, cols]
             turned = jnp.concatenate([real * cosine - imag * sine, real * sine + imag * cosine], 1)
-            bh[c * n1 : (c + 1) * n1], bl[c * n1 : (c + 1) * n1] = split(turned)
+            bh[k * n1 : (k + 1) * n1], bl[k * n1 : (k + 1) * n1] = split(turned)
         high, low = bh[...], bl[...]
         spec[base] = mm(high, fwdh_ref[...]) + mm(low, fwdh_ref[...]) + mm(high, fwdl_ref[...])
 
     def synthesize(real, imag):
+        count = real.shape[0] // n1
         high, low = split(jnp.concatenate([real, imag], 1))
         stage = mm(high, bckh_ref[...]) + mm(low, bckh_ref[...]) + mm(high, bckl_ref[...])
-        for c in range(mine):
-            part = stage[c * n1 : (c + 1) * n1]
+        for k in range(count):
+            part = stage[k * n1 : (k + 1) * n1]
             real, imag = part[:, :LANES], part[:, LANES:]
             turned = jnp.concatenate([real * cosine + imag * sine, imag * cosine - real * sine], 0)
-            cols = slice(c * LANES, (c + 1) * LANES)
+            cols = slice(k * LANES, (k + 1) * LANES)
             zh[:, cols], zl[:, cols] = split(turned)
-        high, low = zh[...], zl[...]
+        high, low = zh[:, : count * LANES], zl[:, : count * LANES]
         result = mm(lasth_ref[...], high) + mm(lasth_ref[...], low) + mm(lastl_ref[...], high)
-        for c in range(mine):
+        turns = count // pair
+        for k in range(count):
+            start = (k % pair) * turns * folds + (k // pair) * folds
             for h in range(folds):
-                rows[pl.ds(c * folds + h, shards, stride=mine * folds), :] = result[
-                    h * shards : (h + 1) * shards, c * LANES : (c + 1) * LANES
+                rows[pl.ds(start + h, shards, stride=count * folds), :] = result[
+                    h * shards : (h + 1) * shards, k * LANES : (k + 1) * LANES
                 ]
-        return rows[...].reshape(shards, mine * folds, LANES).astype(BF16)
-
-    def parts(k):
-        return spec[k, :, :LANES], spec[k, :, LANES:]
+        return rows[: shards * count * folds].reshape(shards, count * folds, LANES).astype(BF16)
+
+    def parts(k, top):
+        span_rows = slice(top * pair * n1, (top + 1) * pair * n1)
+        return spec[k, span_rows, :LANES], spec[k, span_rows, LANES:]
+
+    def publish(g):
+        rows[: group * folds] = mx_recv[g].astype(F32).reshape(group * folds, LANES)
+        mixed = jnp.concatenate([rows[pl.ds(h, group, stride=folds), :] for h in range(folds)], 1)
+        band = slice(g * group, (g + 1) * group)
+        ag_send[g] = jnp.transpose(mixed * gate_ref[band, :].astype(F32)).astype(BF16)
+        def outward():
+            along(ag_send.at[g], ag_recv.at[g, 1], 16 + g, far).start()
+
+        outward()
+
+        @pl.when(inner)
+        def _():
+            along(ag_send.at[g], ag_recv.at[g, 2], 18 + g, opposite).start()
+
+        along(ag_send.at[g], ag_recv.at[g, 0], 11 + g, mate).start()
+        ggrad_ref[band, :] = grad_out[band, :] * mixed
 
     along(rs_send.at[0], rs_recv.at[0], 8, mate).wait_recv()
     along(rs_send.at[1], rs_recv.at[1], 9, mate).wait_recv()
@@ -272,74 +306,78 @@
         grad_out[...] = grad_out[...] + rs_recv[2].astype(F32)
 
     total = grad_out[...]
-    gr_send[...] = to_rows(total * gate_ref[...].astype(F32))
-    joint(in_send, in_recv, 0).wait_send()
+    grads = total * gate_ref[...].astype(F32)
+    gr_send[...] = to_rows([grads[piece(g, h)] for g in range(2) for h in range(folds)])
+    joint(in_send.at[0], in_recv.at[0], 0).wait_send()
+    joint(in_send.at[1], in_recv.at[1], 1).wait_send()
     spread(gr_send, gr_recv, 3)
 
-    joint(in_send, in_recv, 0).wait_recv()
-    analyse(in_recv[:, 0], 0)
-    analyse(in_recv[:, 1], 1)
-    (sr, si), (fr, fi) = parts(0), parts(1)
-    mx_send[...] = synthesize(sr * fr - si * fi, sr * fi + si * fr)
-    spread(mx_send, mx_recv, 2)
+    joint(in_send.at[0], in_recv.at[0], 0).wait_recv()
+    analyse(in_recv[0], 0)
+    (sr, si), (fr, fi) = parts(0, 0), parts(0, 1)
+    mx_send[0] = synthesize(sr * fr - si * fi, sr * fi + si * fr)
+    spread(mx_send.at[0], mx_recv.at[0], 2)
+
+    joint(in_send.at[1], in_recv.at[1], 1).wait_recv()
+    analyse(in_recv[1], 1)
+    (sr, si), (fr, fi) = parts(1, 0), parts(1, 1)
+    mx_send[1] = synthesize(sr * fr - si * fi, sr * fi + si * fr)
+    spread(mx_send.at[1], mx_recv.at[1], 14)
 
     joint(gr_send, gr_recv, 3).wait_recv()
     analyse(gr_recv[...], 2)
-    gr, gi = parts(2)
-    fr, fi = parts(1)
-    rt_send[0] = synthesize(gr * fr + gi * fi, gi * fr - gr * fi)
-    spread(rt_send.at[0], rt_recv.at[0], 5)
-    sr, si = parts(0)
-    gr, gi = parts(2)
-    rt_send[1] = synthesize(gr * sr + gi * si, gi * sr - gr * si)
-    spread(rt_send.at[1], rt_recv.at[1], 4)
-
-    joint(mx_send, mx_recv, 2).wait_recv()
-    mixed = jnp.concatenate(from_rows(mx_recv[...]), 1)
-    ag_send[...] = jnp.transpose(mixed * gate_ref[...].astype(F32)).astype(BF16)
-    for h, cut in enumerate(cuts):
-        along(ag_send.at[cut], ag_recv.at[1, cut], 11 + h, far).start()
-
-    @pl.when(inner)
-    def _():
-        along(ag_send, ag_recv.at[2], 14, opposite).start()
-
-    along(ag_send, ag_recv.at[0], 13, mate).start()
-    ggrad_ref[...] = grad_out[...] * mixed
-
-    for h, cut in enumerate(cuts):
-        along(ag_send.at[cut], ag_recv.at[1, cut], 11 + h, far).wait_recv()
+    for u in range(2):
+        terms = []
+        for g in range(2):
+            (gr, gi), (hr, hi) = parts(2, g), parts(g, 1 - u)
+            terms.append((gr * hr + gi * hi, gi * hr - gr * hi))
+        rt_send[u] = synthesize(*(jnp.concatenate(pieces, 0) for pieces in zip(*terms)))
+        spread(rt_send.at[u], rt_recv.at[u], 5 - u)
+
+    joint(mx_send.at[0], mx_recv.at[0], 2).wait_recv()
+    publish(0)
+
+    joint(mx_send.at[1], mx_recv.at[1], 14).wait_recv()
+    publish(1)
+
+    @pl.when(inner)
+    def _():
+        for g in range(2):
+            along(ag_send.at[g], ag_recv.at[g, 1], 16 + g, far).wait_recv()
+            along(ag_recv.at[g, 1], ag_recv.at[g, 2], 20 + g, mate).start()
+
+    @pl.when(jnp.logical_not(inner))
+    def _():
+        for g in range(2):
+            along(ag_send.at[g], ag_recv.at[g, 1], 16 + g, far).wait_recv()
+
+    def project(g, block, gathered):
+        start = pl.multiple_of(block * wide + g * group, group)
+        return mm(gathered, weight_ref[pl.ds(start, group), :])
+
+    total = project(0, ch, ag_send[0]) + project(1, ch, ag_send[1])
+    for g in range(2):
+        along(ag_send.at[g], ag_recv.at[g, 0], 11 + g, mate).wait_recv()
+        total = total + project(g, mate, ag_recv[g, 0]) + project(g, far, ag_recv[g, 1])
+    for g in range(2):
 
         @pl.when(inner)
         def _():
-            along(ag_recv.at[1, cut], ag_recv.at[2, cut], 15, mate).start()
-
-    def project(block, gathered):
-        part = weight_ref[pl.ds(pl.multiple_of(block * wide, wide), wide), :]
-        return mm(gathered, part)
-
-    total = project(ch, ag_send[...]) + project(far, ag_recv[1])
-    along(ag_send, ag_recv.at[0], 13, mate).wait_recv()
-    total = total + project(mate, ag_recv[0])
-
-    @pl.when(inner)
-    def _():
-        along(ag_send, ag_recv.at[2], 14, opposite).wait_recv()
-
-    @pl.when(jnp.logical_not(inner))
-    def _():
-        along(ag_send, ag_recv.at[2], 15, mate).wait_recv()
-
-    total = total + project(opposite, ag_recv[2])
+            along(ag_send.at[g], ag_recv.at[g, 2], 18 + g, opposite).wait_recv()
+
+        @pl.when(jnp.logical_not(inner))
+        def _():
+            along(ag_send.at[g], ag_recv.at[g, 2], 20 + g, mate).wait_recv()
+
+        total = total + project(g, opposite, ag_recv[g, 2])
     out_ref[...] = total.astype(BF16)
 
     joint(rt_send.at[0], rt_recv.at[0], 5).wait_recv()
-    for h, value in enumerate(from_rows(rt_recv[0])):
-        sgrad_ref[:, h * LANES : (h + 1) * LANES] = value
+    for spot, value in from_rows(rt_recv[0]):
+        sgrad_ref[spot] = value
     joint(rt_send.at[1], rt_recv.at[1], 4).wait_recv()
-    for h, value in enumerate(from_rows(rt_recv[1])):
-        cols = slice(h * LANES, (h + 1) * LANES)
-        tgrad_ref[:, cols] = value * window[:, cols]
+    for spot, value in from_rows(rt_recv[1]):
+        tgrad_ref[spot] = value * window[spot]
 
     along(rs_send.at[0], rs_recv.at[0], 8, mate).wait_send()
 
@@ -354,16 +392,18 @@
         for h, cut in enumerate(cuts):
             along(rs_send.at[2, cut], rs_relay.at[cut], 6 + h, mate).wait_send()
 
-    joint(mx_send, mx_recv, 2).wait_send()
+    joint(mx_send.at[0], mx_recv.at[0], 2).wait_send()
+    joint(mx_send.at[1], mx_recv.at[1], 14).wait_send()
     joint(gr_send, gr_recv, 3).wait_send()
-    for h, cut in enumerate(cuts):
-        along(ag_send.at[cut], ag_recv.at[1, cut], 11 + h, far).wait_send()
-    along(ag_send, ag_recv.at[0], 13, mate).wait_send()
-
-    @pl.when(inner)
-    def _():
-        along(ag_send, ag_recv.at[2], 14, mate).wait_send()
-        along(ag_recv.at[1], ag_recv.at[2], 15, mate).wait_send()
+    for g in range(2):
+        along(ag_send.at[g], ag_recv.at[g, 0], 11 + g, mate).wait_send()
+        along(ag_send.at[g], ag_recv.at[g, 1], 16 + g, far).wait_send()
+
+    @pl.when(inner)
+    def _():
+        for g in range(2):
+            along(ag_send.at[g], ag_recv.at[g, 2], 18 + g, opposite).wait_send()
+            along(ag_recv.at[g, 1], ag_recv.at[g, 2], 20 + g, mate).wait_send()
 
     joint(rt_send.at[0], rt_recv.at[0], 5).wait_send()
     joint(rt_send.at[1], rt_recv.at[1], 4).wait_send()
@@ -411,18 +451,18 @@
         in_specs=[away] * (6 + len(consts)),
         out_specs=(vmem,) * 4,
         scratch_shapes=[
-            pltpu.VMEM((shards, 2, *tile), BF16),
-            pltpu.VMEM((shards, 2, *tile), BF16),
+            pltpu.VMEM((2, shards, *tile), BF16),
+            pltpu.VMEM((2, shards, *tile), BF16),
             pltpu.VMEM((chans - 1, wide, span), BF16),
             pltpu.VMEM((chans - 1, wide, span), BF16),
-            pltpu.VMEM((shards, *tile), BF16),
-            pltpu.VMEM((shards, *tile), BF16),
+            pltpu.VMEM((2, shards, tile[0] // 2, LANES), BF16),
+            pltpu.VMEM((2, shards, tile[0] // 2, LANES), BF16),
             pltpu.VMEM((shards, *tile), BF16),
             pltpu.VMEM((shards, *tile), BF16),
             pltpu.VMEM((2, shards, *tile), BF16),
             pltpu.VMEM((2, shards, *tile), BF16),
-            pltpu.VMEM((span, wide), BF16),
-            pltpu.VMEM((chans - 1, span, wide), BF16),
+            pltpu.VMEM((2, span, wide // 2), BF16),
+            pltpu.VMEM((2, chans - 1, span, wide // 2), BF16),
             pltpu.VMEM((wide, span), BF16),
             pltpu.VMEM((wide, span), F32),
             pltpu.VMEM((wide * folds, LANES), F32),
@@ -437,8 +477,8 @@
             *(pltpu.VMEM(x.shape, x.dtype) for x in (signal, gating, filter_taps)),
             pltpu.VMEM((wide // LANES, LANES), F32),
             *(pltpu.VMEM(x.shape, x.dtype) for x in (out_weight, out_grad, *consts)),
-            pltpu.SemaphoreType.DMA((16,)),
-            pltpu.SemaphoreType.DMA((16,)),
+            pltpu.SemaphoreType.DMA((22,)),
+            pltpu.SemaphoreType.DMA((22,)),
             pltpu.SemaphoreType.DMA((9,)),
             pltpu.SemaphoreType.REGULAR,
             pltpu.SemaphoreType.REGULAR,

time: 53.7 us -> 51.4 us (0.957)
  Pallas kernels: 53 us -> 50.7 us
    pallas_call x1, Pallas kernels: 52 us -> 49.7 us  [per_device(): pl.pallas_call(functools.partial(body, shards, chans), out_shape=(jax.Sha...]
where the time goes in v4:
time: 51.4 us; the launch traced here: 51.3 us
  Pallas kernels  50.7 us (99%)
  between operations  0.64 us (1%)
    pallas_call x1, Pallas kernels, per_device(): pl.pallas_call(functools.partial(body, shards, chans), out_shape=(jax.Sha...  49.7 us

profile of v4, /device:TPU:1, one launch (start us, length us, event | category | flops | bytes accessed | tf_op | source)
XLA Modules:
  0.0 51.3 jit_solution(7746897882994123374)
XLA Ops:
  0.6 49.7 %shard_map.120 = (bf16[256,512]{1,0:T(8,128)(2,1)S(1)}, f32[256,256]{1,0:T(8,128)S(1)}, f32[256,256]{1,0:T(8,128)S(1)}, f32[256,256]{1,0:T(8,128)S(1)}) custom-call(bf16[256,256]{1,0:T(8,128)(2,1)} %sig_hbm.1, bf16[256,256]{1,0:T(8,128)(2,1)} %gate_hbm.1, f32[256,256]{1,0:T(8,128)} %taps_hbm.1, f32[2,128]{1,0:T(2,128)} %bitcast.1, ...), custom_call_target="tpu_custom_call" | custom-call | tf_op jit(solution)/shard_map/pallas_call | solution.py:443
  50.3 1.0 %shard_map.121 = (bf16[256,512]{1,0:T(8,128)(2,1)}, f32[256,256]{1,0:T(8,128)}, f32[256,256]{1,0:T(8,128)}, f32[256,256]{1,0:T(8,128)}) custom-call(bf16[256,512]{1,0:T(8,128)(2,1)S(1)} %get-tuple-element.8.refs_0_, f32[256,256]{1,0:T(8,128)S(1)} %get-tuple-element.9.refs_1_, f32[256,256]{1,0:T(8,128)S(1)} %get-tuple-element.10.refs_2_, ...), custom_call_target="tpu_custom_call" | custom-call | tf_op jit(solution)/shard_map/pallas_call | solution.py:425

commit v5 on v4

--- a/solution.py
+++ b/solution.py
@@ -250,14 +250,14 @@
             cols = slice(k * LANES, (k + 1) * LANES)
             real, imag = stage[:n1, cols], stage[n1:, cols]
             turned = jnp.concatenate([real * cosine - imag * sine, real * sine + imag * cosine], 1)
-            bh[k * n1 : (k + 1) * n1], bl[k * n1 : (k + 1) * n1] = split(turned)
-        high, low = bh[...], bl[...]
-        spec[base] = mm(high, fwdh_ref[...]) + mm(low, fwdh_ref[...]) + mm(high, fwdl_ref[...])
+            bh[k * n1 : (k + 1) * n1] = turned.astype(BF16)
+        high = bh[...]
+        spec[base] = mm(high, fwdh_ref[...]) + mm(high, fwdl_ref[...])
 
     def synthesize(real, imag):
         count = real.shape[0] // n1
-        high, low = split(jnp.concatenate([real, imag], 1))
-        stage = mm(high, bckh_ref[...]) + mm(low, bckh_ref[...]) + mm(high, bckl_ref[...])
+        high = jnp.concatenate([real, imag], 1).astype(BF16)
+        stage = mm(high, bckh_ref[...]) + mm(high, bckl_ref[...])
         for k in range(count):
             part = stage[k * n1 : (k + 1) * n1]
             real, imag = part[:, :LANES], part[:, LANES:]
@@ -355,29 +355,29 @@
         start = pl.multiple_of(block * wide + g * group, group)
         return mm(gathered, weight_ref[pl.ds(start, group), :])
 
-    total = project(0, ch, ag_send[0]) + project(1, ch, ag_send[1])
-    for g in range(2):
-        along(ag_send.at[g], ag_recv.at[g, 0], 11 + g, mate).wait_recv()
-        total = total + project(g, mate, ag_recv[g, 0]) + project(g, far, ag_recv[g, 1])
-    for g in range(2):
-
-        @pl.when(inner)
-        def _():
-            along(ag_send.at[g], ag_recv.at[g, 2], 18 + g, opposite).wait_recv()
-
-        @pl.when(jnp.logical_not(inner))
-        def _():
-            along(ag_send.at[g], ag_recv.at[g, 2], 20 + g, mate).wait_recv()
-
-        total = total + project(g, opposite, ag_recv[g, 2])
-    out_ref[...] = total.astype(BF16)
-
     joint(rt_send.at[0], rt_recv.at[0], 5).wait_recv()
     for spot, value in from_rows(rt_recv[0]):
         sgrad_ref[spot] = value
     joint(rt_send.at[1], rt_recv.at[1], 4).wait_recv()
     for spot, value in from_rows(rt_recv[1]):
         tgrad_ref[spot] = value * window[spot]
+
+    total = project(0, ch, ag_send[0]) + project(1, ch, ag_send[1])
+    for g in range(2):
+        along(ag_send.at[g], ag_recv.at[g, 0], 11 + g, mate).wait_recv()
+        total = total + project(g, mate, ag_recv[g, 0]) + project(g, far, ag_recv[g, 1])
+    for g in range(2):
+
+        @pl.when(inner)
+        def _():
+            along(ag_send.at[g], ag_recv.at[g, 2], 18 + g, opposite).wait_recv()
+
+        @pl.when(jnp.logical_not(inner))
+        def _():
+            along(ag_send.at[g], ag_recv.at[g, 2], 20 + g, mate).wait_recv()
+
+        total = total + project(g, opposite, ag_recv[g, 2])
+    out_ref[...] = total.astype(BF16)
 
     along(rs_send.at[0], rs_recv.at[0], 8, mate).wait_send()
 

time: 51.4 us -> 50.9 us (level)
  Pallas kernels: 50.7 us -> 50.1 us
    pallas_call x1, Pallas kernels: 49.7 us -> 49.1 us  [per_device(): pl.pallas_call(functools.partial(body, shards, chans), out_shape=(jax.Sha...]
where the time goes in v5:
time: 50.9 us; the launch traced here: 50.8 us
  Pallas kernels  50.1 us (98%)
  between operations  0.64 us (1%)
    pallas_call x1, Pallas kernels, per_device(): pl.pallas_call(functools.partial(body, shards, chans), out_shape=(jax.Sha...  49.1 us

profile of v5, /device:TPU:1, one launch (start us, length us, event | category | flops | bytes accessed | tf_op | source)
XLA Modules:
  0.0 50.8 jit_solution(5428915606520990945)
XLA Ops:
  0.6 49.1 %shard_map.120 = (bf16[256,512]{1,0:T(8,128)(2,1)S(1)}, f32[256,256]{1,0:T(8,128)S(1)}, f32[256,256]{1,0:T(8,128)S(1)}, f32[256,256]{1,0:T(8,128)S(1)}) custom-call(bf16[256,256]{1,0:T(8,128)(2,1)} %sig_hbm.1, bf16[256,256]{1,0:T(8,128)(2,1)} %gate_hbm.1, f32[256,256]{1,0:T(8,128)} %taps_hbm.1, f32[2,128]{1,0:T(2,128)} %bitcast.1, ...), custom_call_target="tpu_custom_call" | custom-call | tf_op jit(solution)/shard_map/pallas_call | solution.py:443
  49.8 1.0 %shard_map.121 = (bf16[256,512]{1,0:T(8,128)(2,1)}, f32[256,256]{1,0:T(8,128)}, f32[256,256]{1,0:T(8,128)}, f32[256,256]{1,0:T(8,128)}) custom-call(bf16[256,512]{1,0:T(8,128)(2,1)S(1)} %get-tuple-element.8.refs_0_, f32[256,256]{1,0:T(8,128)S(1)} %get-tuple-element.9.refs_1_, f32[256,256]{1,0:T(8,128)S(1)} %get-tuple-element.10.refs_2_, ...), custom_call_target="tpu_custom_call" | custom-call | tf_op jit(solution)/shard_map/pallas_call | solution.py:425
